TPU v7x, 128 devices: a whole 4x4x4 slice. The times are simulated.
128 devices in a mesh: row: 16 (over x, z), col: 8 (over y, core).
Axes of the slice: x: 4, y: 4, z: 4, core: 2. Of those that a mesh axis runs over, the one named last changes fastest.
Arguments:
- block_values: bfloat16 [16, 8, 256, 128, 128], P('row', 'col')
- block_rows: int32 [16, 8, 256], P('row', 'col'), may hold values from -1 to 511, as said below
- block_cols: int32 [16, 8, 256], P('row', 'col'), may hold values from -1 to 511, as said below
- cost_vec: float32 [524288], P('col')
- demand: float32 [1048576], P('row')
- lower: float32 [524288], P('col'), may hold values from -1.5 to -0.2
- upper: float32 [524288], P('col'), may hold values from 0.2 to 1.5
- bound_kind: int32 [524288], P('col'), may hold values from 0 to 3
- primal_start: float32 [524288], P('col'), may hold values from -4 to 4
- dual_start: float32 [1048576], P('row'), may hold values from 0 to 1.5
Outputs:
- primal_out: float32 [524288], P('col')
- dual_out: float32 [1048576], P('row')
Inputs may be any that keep to these rules, and one draw needn't show every extreme that they name: A slot's block_rows and block_cols are both -1 exactly when the slot is empty; the live slots of a device come first, a device has at least 64 of them, and in every draw some device has all 256 slots live and some device has empty slots; every block row and every block column of the whole matrix is named by some live slot; a block place may be named by several slots. `block_cols`: as for block_rows.
All inputs are finite; a program needn't handle non-finite values.
Results may differ from a plain program's by a relative error of at most 0.0073.
Values sent between devices are 32-bit elements; how exact they have to be, the bound alone decides.
A program may use at most 64 MiB of HBM per device.

v0:
```python
import jax
import jax.numpy as jnp
from jax import lax
from jax.sharding import PartitionSpec as P

RUIZ_PASSES = 2
ITERS = 2
SMALL_EPS = 1e-06
STEP_SCALE = 0.3


def pick_tiles(vector, slot_ids, tile_count):
    tile_width = vector.shape[0] // tile_count
    padded = jnp.concatenate(
        [vector.reshape(tile_count, tile_width), jnp.zeros((1, tile_width), vector.dtype)], axis=0
    )
    return padded[slot_ids]


def tile_peaks(block_terms, slot_ids, tile_count):
    tile_width = block_terms.shape[1]
    return (
        jnp.zeros((tile_count + 1, tile_width), jnp.float32)
        .at[slot_ids]
        .max(block_terms)[:tile_count]
        .reshape(-1)
    )


def tile_sums(block_terms, slot_ids, tile_count):
    tile_width = block_terms.shape[1]
    return (
        jnp.zeros((tile_count + 1, tile_width), jnp.float32)
        .at[slot_ids]
        .add(block_terms)[:tile_count]
        .reshape(-1)
    )


def project_bounds(values, low_side, high_side, bound_types):
    lifted = jnp.where(
        (bound_types == 1) | (bound_types == 3), jnp.maximum(values, low_side), values
    )
    return jnp.where(
        (bound_types == 2) | (bound_types == 3), jnp.minimum(lifted, high_side), lifted
    )


def per_device(
    block_values,
    block_rows,
    block_cols,
    cost_vec,
    demand,
    lower,
    upper,
    bound_kind,
    primal_start,
    dual_start,
):
    values = block_values[0, 0]
    row_ids = block_rows[0, 0]
    col_ids = block_cols[0, 0]
    tile_width = values.shape[1]
    row_length = demand.shape[0]
    col_length = cost_vec.shape[0]
    row_count = row_length // tile_width
    col_count = col_length // tile_width
    live_slot = row_ids >= 0
    row_slot = jnp.where(live_slot, row_ids, row_count)
    col_slot = jnp.where(live_slot, col_ids, col_count)
    row_scale = jnp.ones((row_length,), jnp.float32)
    col_scale = jnp.ones((col_length,), jnp.float32)
    for pass_index in range(RUIZ_PASSES):
        row_part = pick_tiles(row_scale, row_slot, row_count)
        col_part = pick_tiles(col_scale, col_slot, col_count)
        scaled = jnp.abs(values).astype(jnp.float32) * row_part[:, :, None] * col_part[:, None, :]
        row_peak = lax.pmax(tile_peaks(jnp.max(scaled, axis=2), row_slot, row_count), "col")
        col_peak = lax.pmax(tile_peaks(jnp.max(scaled, axis=1), col_slot, col_count), "row")
        row_scale = row_scale / jnp.sqrt(row_peak + SMALL_EPS)
        col_scale = col_scale / jnp.sqrt(col_peak + SMALL_EPS)
    scaled_cost = col_scale * cost_vec
    scaled_demand = row_scale * demand
    cost_square = jnp.sum(scaled_cost * scaled_cost)
    demand_square = jnp.sum(scaled_demand * scaled_demand)
    cost_total = lax.psum(cost_square, "col")
    demand_total = lax.psum(demand_square, "row")
    norm_ratio = jnp.sqrt(cost_total + SMALL_EPS) / jnp.sqrt(demand_total + SMALL_EPS)
    primal_step = STEP_SCALE / norm_ratio
    dual_step = STEP_SCALE * norm_ratio
    primal = primal_start / col_scale
    dual_now = dual_start / row_scale
    low_side = lower / col_scale
    high_side = upper / col_scale
    for pass_index in range(ITERS):
        weights = (row_scale * dual_now).astype(jnp.bfloat16)
        picked = pick_tiles(weights, row_slot, row_count)
        partial_value = tile_sums(
            jnp.einsum("kij,ki->kj", values, picked, preferred_element_type=jnp.float32),
            col_slot,
            col_count,
        )
        gradient = col_scale * lax.psum(partial_value, "row")
        primal_next = project_bounds(
            primal - primal_step * (scaled_cost - gradient), low_side, high_side, bound_kind
        )
        shifted = (col_scale * (2.0 * primal_next - primal)).astype(jnp.bfloat16)
        picked = pick_tiles(shifted, col_slot, col_count)
        partial_value = tile_sums(
            jnp.einsum("kij,kj->ki", values, picked, preferred_element_type=jnp.float32),
            row_slot,
            row_count,
        )
        row_image = row_scale * lax.psum(partial_value, "col")
        dual_now = jnp.maximum(dual_now + dual_step * (scaled_demand - row_image), 0.0)
        primal = primal_next
    return (col_scale * primal, row_scale * dual_now)


def solution(mesh):
    return jax.shard_map(
        per_device,
        mesh=mesh,
        in_specs=(
            P("row", "col", None, None, None),
            P("row", "col", None),
            P("row", "col", None),
            P("col"),
            P("row"),
            P("col"),
            P("col"),
            P("col"),
            P("col"),
            P("row"),
        ),
        out_specs=(P("col"), P("row")),
        check_vma=False,
    )
```

profile of v0, /device:TPU:0, one launch (start us, length us, event | category | flops | bytes accessed | tf_op | source)
XLA Modules:
  0.0 671.1 jit_solution(2063073004390619092)
XLA Ops:
  9.6 12.0 %fusion.1 = (f32[256,128]{1,0:T(8,128)S(1)}, f32[256,128]{1,0:T(8,128)S(1)}) fusion(f32[256,128]{1,0:T(8,128)S(1)} %gather_fusion.1, f32[256,128]{1,0:T(8,128)S(1)} %gather_fusion, bf16[1,1,256,128,128]{4,3,2,1,0:T(8,128)(2,1)} %param.10), kind=kLoop, calls=%fused_computation.19 | loop fusion | flops 25100288 | bytes 8912896 | tf_op jit(solution)/shard_map/reduce_max | solution.py:78
  21.5 1.7 scatter_custom_fusion.1
  26.5 60.2 %all-reduce.18.cloned.1.call-done = f32[65536]{0:T(1024)} async-done(((f32[65536]{0:T(1024)}), f32[65536]{0:T(1024)}) %all-reduce.18.cloned.1.call-update) | async-done | bytes 262160 | tf_op jit(solution)/shard_map/pmax | solution.py:78
  88.6 85.9 %all-reduce.16.cloned.1.call-done = f32[65536]{0:T(1024)} async-done(((f32[65536]{0:T(1024)}), f32[65536]{0:T(1024)}) %all-reduce.16.cloned.1.call-update) | async-done | bytes 262160 | tf_op jit(solution)/shard_map/pmax | solution.py:79
  176.2 11.9 %fusion.4 = (f32[256,128]{1,0:T(8,128)S(1)}, f32[256,128]{1,0:T(8,128)S(1)}) fusion(f32[256,128]{1,0:T(8,128)S(1)} %gather_fusion.3, f32[256,128]{1,0:T(8,128)S(1)} %gather_fusion.2, bf16[1,1,256,128,128]{4,3,2,1,0:T(8,128)(2,1)} %param.10), kind=kLoop, calls=%fused_computation.22 | loop fusion | flops 25100288 | bytes 8912896 | tf_op jit(solution)/shard_map/reduce_max | solution.py:78
  193.1 56.8 %all-reduce.22.cloned.1.call-done = f32[65536]{0:T(1024)} async-done(((f32[65536]{0:T(1024)}), f32[65536]{0:T(1024)}) %all-reduce.22.cloned.1.call-update) | async-done | bytes 262160 | tf_op jit(solution)/shard_map/pmax | solution.py:78
  249.9 1.7 multiply_reduce_fusion
  252.6 5.6 fusion.12
  258.2 1.7 scatter_custom_fusion.4
  260.7 40.9 %psum.43 = f32[]{:T(128)} all-reduce(f32[]{:T(128)} %get-tuple-element.12), channel_id=1, replica_groups=mesh['row'=16,'col'=8] {'row'}, use_global_device_ids=true, to_apply=%region_15.16 | all-reduce | flops 1 | bytes 8 | tf_op jit(solution)/shard_map/psum | solution.py:87
  302.3 35.2 %all-reduce.20.cloned.1.call-done = f32[65536]{0:T(1024)} async-done(((f32[65536]{0:T(1024)}), f32[65536]{0:T(1024)}) %all-reduce.20.cloned.1.call-update) | async-done | bytes 262160 | tf_op jit(solution)/shard_map/pmax | solution.py:79
  339.2 14.1 %psum.42 = f32[]{:T(128)} all-reduce(f32[]{:T(128)} %get-tuple-element.15), channel_id=1, replica_groups=mesh['row'=16,'col'=8] {'col'}, use_global_device_ids=true, to_apply=%region_10.11 | all-reduce | flops 1 | bytes 8 | tf_op jit(solution)/shard_map/psum | solution.py:86
  354.0 70.8 %all-reduce.24.cloned.1.call-done = f32[65536]{0:T(1024)} async-done(((f32[65536]{0:T(1024)}), f32[65536]{0:T(1024)}) %all-reduce.24.cloned.1.call-update) | async-done | bytes 262160 | tf_op jit(solution)/shard_map/psum | solution.py:103
  426.9 7.8 %fusion.10 = f32[256,1,128]{2,1,0:T(1,128)S(1)} fusion(bf16[1,1,256,128,128]{4,3,2,1,0:T(8,128)(2,1)} %param.10, bf16[256,128,1]{1,0,2:T(8,128)(2,1)S(1)} %bitcast.68), kind=kOutput, calls=%fused_computation.28 | convolution fusion | flops 8388608 | bytes 8585216 | tf_op jit(solution)/shard_map/kij,kj->ki/dot_general | solution.py:110
  434.6 1.7 scatter_custom_fusion.5
  437.1 59.2 %all-reduce.26.cloned.1.call-done = f32[65536]{0:T(1024)} async-done(((f32[65536]{0:T(1024)}), f32[65536]{0:T(1024)}) %all-reduce.26.cloned.1.call-update) | async-done | bytes 262160 | tf_op jit(solution)/shard_map/psum | solution.py:114
  498.2 5.7 fusion.8
  503.9 1.7 scatter_custom_fusion.6
  506.4 83.9 %all-reduce.28.cloned.1.call-done = f32[65536]{0:T(1024)} async-done(((f32[65536]{0:T(1024)}), f32[65536]{0:T(1024)}) %all-reduce.28.cloned.1.call-update) | async-done | bytes 262160 | tf_op jit(solution)/shard_map/psum | solution.py:103
  590.3 1.9 fusion.40
  593.0 7.8 %fusion.6 = f32[256,1,128]{2,1,0:T(1,128)S(1)} fusion(bf16[1,1,256,128,128]{4,3,2,1,0:T(8,128)(2,1)} %param.10, bf16[256,128,1]{1,0,2:T(8,128)(2,1)S(1)} %bitcast.66), kind=kOutput, calls=%fused_computation.24 | convolution fusion | flops 8388608 | bytes 8585216 | tf_op jit(solution)/shard_map/kij,kj->ki/dot_general | solution.py:110
  600.8 1.7 scatter_custom_fusion.7
  603.3 59.2 %all-reduce.30.cloned.1.call-done = f32[65536]{0:T(1024)} async-done(((f32[65536]{0:T(1024)}), f32[65536]{0:T(1024)}) %all-reduce.30.cloned.1.call-update) | async-done | bytes 262160 | tf_op jit(solution)/shard_map/psum | solution.py:114
  662.5 1.8 maximum_multiply_fusion
  (75 shorter events, 24.5 us)
Async XLA Ops:
  7.2 79.6 %all-reduce.18.cloned.1.call-start = ((), (), s32[]{:S(2)}) async-start(), calls=%async_computation.1 | async-start | bytes 524288 | tf_op jit(solution)/shard_map/pmax | solution.py:78
  23.9 226.0 %copy-start.4 = (f32[65536]{0:T(1024)S(1)}, f32[65536]{0:T(1024)}, u32[]{:S(2)}) copy-start(f32[65536]{0:T(1024)} %param.14) | copy-start | bytes 786436
  24.0 150.5 %all-reduce.16.cloned.1.call-start = ((), (), s32[]{:S(2)}) async-start(), calls=%async_computation | async-start | bytes 524288 | tf_op jit(solution)/shard_map/pmax | solution.py:79
  26.4 225.2 %copy-start.5 = (f32[65536]{0:T(1024)S(1)}, f32[65536]{0:T(1024)}, u32[]{:S(2)}) copy-start(f32[65536]{0:T(1024)} %param.19) | copy-start | bytes 786436
  26.4 223.5 %all-reduce.22.cloned.1.call-start = ((), (), s32[]{:S(2)}) async-start(), calls=%async_computation.3 | async-start | bytes 524288 | tf_op jit(solution)/shard_map/pmax | solution.py:78
  86.7 163.2 %copy-start.2 = (f32[65536]{0:T(1024)S(1)}, f32[65536]{0:T(1024)}, u32[]{:S(2)}) copy-start(f32[65536]{0:T(1024)} %all-reduce.18.cloned.1.call-done) | copy-start | bytes 786436
  188.1 149.4 %copy-start.1 = (f32[65536]{0:T(1024)S(1)}, f32[65536]{0:T(1024)}, u32[]{:S(2)}) copy-start(f32[65536]{0:T(1024)} %all-reduce.16.cloned.1.call-done) | copy-start | bytes 786436
  188.1 149.4 %copy-start.6 = (f32[65536]{0:T(1024)S(1)}, f32[65536]{0:T(1024)}, u32[]{:S(2)}) copy-start(f32[65536]{0:T(1024)} %param.13) | copy-start | bytes 786436
  188.1 236.6 %copy-start.7 = (f32[65536]{0:T(1024)S(1)}, f32[65536]{0:T(1024)}, u32[]{:S(2)}) copy-start(f32[65536]{0:T(1024)} %param.18) | copy-start | bytes 786436
  188.1 236.6 %copy-start.8 = (f32[65536]{0:T(1024)S(1)}, f32[65536]{0:T(1024)}, u32[]{:S(2)}) copy-start(f32[65536]{0:T(1024)} %param.15) | copy-start | bytes 786436
  188.1 236.6 %copy-start.9 = (s32[65536]{0:T(1024)S(1)}, s32[65536]{0:T(1024)}, u32[]{:S(2)}) copy-start(s32[65536]{0:T(1024)} %param.17) | copy-start | bytes 786436
  188.2 236.6 %copy-start.10 = (f32[65536]{0:T(1024)S(1)}, f32[65536]{0:T(1024)}, u32[]{:S(2)}) copy-start(f32[65536]{0:T(1024)} %param.16) | copy-start | bytes 786436
  190.6 146.9 %all-reduce.20.cloned.1.call-start = ((), (), s32[]{:S(2)}) async-start(), calls=%async_computation.2 | async-start | bytes 524288 | tf_op jit(solution)/shard_map/pmax | solution.py:79
  193.1 231.7 %all-reduce.24.cloned.1.call-start = ((), (), s32[]{:S(2)}) async-start(), calls=%async_computation.4 | async-start | bytes 524288 | tf_op jit(solution)/shard_map/psum | solution.py:103
  260.7 235.7 %all-reduce.26.cloned.1.call-start = ((), (), s32[]{:S(2)}) async-start(), calls=%async_computation.5 | async-start | bytes 524288 | tf_op jit(solution)/shard_map/psum | solution.py:114
  434.6 155.7 %copy-start = (f32[65536]{0:T(1024)S(1)}, f32[65536]{0:T(1024)}, u32[]{:S(2)}) copy-start(f32[65536]{0:T(1024)} %all-reduce.24.cloned.1.call-done) | copy-start | bytes 786436
  437.1 153.2 %all-reduce.28.cloned.1.call-start = ((), (), s32[]{:S(2)}) async-start(), calls=%async_computation.6 | async-start | bytes 524288 | tf_op jit(solution)/shard_map/psum | solution.py:103
  503.9 158.6 %copy-start.3 = (f32[65536]{0:T(1024)S(1)}, f32[65536]{0:T(1024)}, u32[]{:S(2)}) copy-start(f32[65536]{0:T(1024)} %all-reduce.26.cloned.1.call-done) | copy-start | bytes 786436
  506.3 156.2 %all-reduce.30.cloned.1.call-start = ((), (), s32[]{:S(2)}) async-start(), calls=%async_computation.7 | async-start | bytes 524288 | tf_op jit(solution)/shard_map/psum | solution.py:114
Sparse Core Ops, SparseCore 0:
  24.1 62.5 all-reduce.17
  90.8 83.6 all-reduce.15
  190.7 59.1 all-reduce.21
  253.9 83.5 all-reduce.19
  341.1 83.6 all-reduce.23
  437.2 59.0 all-reduce.25
  506.4 83.8 all-reduce.27
  603.4 59.0 all-reduce.29
where the time goes:
time: 672 us; the launch traced here: 671 us
  waiting for transfers between devices  512 us (76%)
  blocking collectives  55 us (8%)
  other arithmetic  49.3 us (7%)
  matrix products  26.9 us (4%)
  between operations  15.8 us (2%)
  local copies, waits for them, and re-layouts  12.4 us (2%)
    psum x2, waiting for transfers between devices, per_device(): gradient = col_scale * lax.psum(partial_value, 'row')  155 us
    pmax x2, waiting for transfers between devices, per_device(): lax.pmax(tile_peaks(jnp.max(scaled, axis=1), col_slot, col_count), 'row')  121 us
    psum x2, waiting for transfers between devices, per_device(): row_image = row_scale * lax.psum(partial_value, 'col')  118 us
    pmax x2, waiting for transfers between devices, per_device(): lax.pmax(tile_peaks(jnp.max(scaled, axis=2), row_slot, row_count), 'col')  117 us
    psum x1, blocking collectives, per_device(): demand_total = lax.psum(demand_square, 'row')  40.9 us
    reduce_max x2, other arithmetic, per_device(): jnp.max(scaled, axis=2)  23.8 us
    dot_general x2, matrix products, per_device(): jnp.einsum('kij,kj->ki', values, picked, preferred_element_type=jnp.float32)  15.6 us
    psum x1, blocking collectives, per_device(): cost_total = lax.psum(cost_square, 'col')  14.1 us
  transfers between devices with their start and end apart: 8, of which 8 were waited for; matrix products, arithmetic and copies ran while one was open for 3% of the time, Pallas kernels for 0%

commit v1 on v0

--- a/solution.py
+++ b/solution.py
@@ -111,7 +111,7 @@
             row_slot,
             row_count,
         )
-        row_image = row_scale * lax.psum(partial_value, "col")
+        row_image = row_scale * jnp.sum(lax.all_gather(partial_value, "col"), axis=0)
         dual_now = jnp.maximum(dual_now + dual_step * (scaled_demand - row_image), 0.0)
         primal = primal_next
     return (col_scale * primal, row_scale * dual_now)

time: 672 us -> 609 us (0.906)
  waiting for transfers between devices: 512 us -> 443 us
    psum x2 -> x0, waiting for transfers between devices: 118 us -> none  [per_device(): row_image = row_scale * lax.psum(partial_value, 'col')]
    all_gather x0 -> x2, waiting for transfers between devices: none -> 49.1 us  [per_device(): lax.all_gather(partial_value, 'col')]
where the time goes in v1:
time: 609 us; the launch traced here: 607 us
  waiting for transfers between devices  443 us (73%)
  blocking collectives  54.9 us (9%)
  other arithmetic  53.7 us (9%)
  matrix products  26.8 us (4%)
  between operations  15.7 us (3%)
  local copies, waits for them, and re-layouts  12.4 us (2%)
    psum x2, waiting for transfers between devices, per_device(): gradient = col_scale * lax.psum(partial_value, 'row')  156 us
    pmax x2, waiting for transfers between devices, per_device(): lax.pmax(tile_peaks(jnp.max(scaled, axis=1), col_slot, col_count), 'row')  121 us
    pmax x2, waiting for transfers between devices, per_device(): lax.pmax(tile_peaks(jnp.max(scaled, axis=2), row_slot, row_count), 'col')  117 us
    all_gather x2, waiting for transfers between devices, per_device(): lax.all_gather(partial_value, 'col')  49.1 us
    psum x1, blocking collectives, per_device(): demand_total = lax.psum(demand_square, 'row')  40.8 us
    reduce_max x2, other arithmetic, per_device(): jnp.max(scaled, axis=2)  23.9 us
    dot_general x2, matrix products, per_device(): jnp.einsum('kij,kj->ki', values, picked, preferred_element_type=jnp.float32)  15.6 us
    psum x1, blocking collectives, per_device(): cost_total = lax.psum(cost_square, 'col')  14.1 us
  transfers between devices with their start and end apart: 8, of which 8 were waited for; matrix products, arithmetic and copies ran while one was open for 3% of the time, Pallas kernels for 0%

profile of v1, /device:TPU:0, one launch (start us, length us, event | category | flops | bytes accessed | tf_op | source)
XLA Modules:
  0.0 607.1 jit_solution(8570681838619352709)
XLA Ops:
  9.6 12.0 %fusion.1 = (f32[256,128]{1,0:T(8,128)S(1)}, f32[256,128]{1,0:T(8,128)S(1)}) fusion(f32[256,128]{1,0:T(8,128)S(1)} %gather_fusion.1, f32[256,128]{1,0:T(8,128)S(1)} %gather_fusion, bf16[1,1,256,128,128]{4,3,2,1,0:T(8,128)(2,1)} %param.10), kind=kLoop, calls=%fused_computation.19 | loop fusion | flops 25100288 | bytes 8912896 | tf_op jit(solution)/shard_map/reduce_max | solution.py:78
  26.5 60.2 %all-reduce.16.cloned.1.call-done = f32[65536]{0:T(1024)} async-done(((f32[65536]{0:T(1024)}), f32[65536]{0:T(1024)}) %all-reduce.16.cloned.1.call-update) | async-done | bytes 262160 | tf_op jit(solution)/shard_map/pmax | solution.py:78
  88.6 85.9 %all-reduce.14.cloned.1.call-done = f32[65536]{0:T(1024)} async-done(((f32[65536]{0:T(1024)}), f32[65536]{0:T(1024)}) %all-reduce.14.cloned.1.call-update) | async-done | bytes 262160 | tf_op jit(solution)/shard_map/pmax | solution.py:79
  176.2 11.9 %fusion.4 = (f32[256,128]{1,0:T(8,128)S(1)}, f32[256,128]{1,0:T(8,128)S(1)}) fusion(f32[256,128]{1,0:T(8,128)S(1)} %gather_fusion.3, f32[256,128]{1,0:T(8,128)S(1)} %gather_fusion.2, bf16[1,1,256,128,128]{4,3,2,1,0:T(8,128)(2,1)} %param.10), kind=kLoop, calls=%fused_computation.22 | loop fusion | flops 25100288 | bytes 8912896 | tf_op jit(solution)/shard_map/reduce_max | solution.py:78
  193.2 56.8 %all-reduce.20.cloned.1.call-done = f32[65536]{0:T(1024)} async-done(((f32[65536]{0:T(1024)}), f32[65536]{0:T(1024)}) %all-reduce.20.cloned.1.call-update) | async-done | bytes 262160 | tf_op jit(solution)/shard_map/pmax | solution.py:78
  250.0 1.7 multiply_reduce_fusion
  252.6 5.6 fusion.12
  258.3 1.7 scatter_custom_fusion.4
  260.8 40.8 %psum.29 = f32[]{:T(128)} all-reduce(f32[]{:T(128)} %get-tuple-element.12), channel_id=1, replica_groups=mesh['row'=16,'col'=8] {'row'}, use_global_device_ids=true, to_apply=%region_15.16 | all-reduce | flops 1 | bytes 8 | tf_op jit(solution)/shard_map/psum | solution.py:87
  302.2 35.4 %all-reduce.18.cloned.1.call-done = f32[65536]{0:T(1024)} async-done(((f32[65536]{0:T(1024)}), f32[65536]{0:T(1024)}) %all-reduce.18.cloned.1.call-update) | async-done | bytes 262160 | tf_op jit(solution)/shard_map/pmax | solution.py:79
  339.2 14.1 %psum.28 = f32[]{:T(128)} all-reduce(f32[]{:T(128)} %get-tuple-element.15), channel_id=1, replica_groups=mesh['row'=16,'col'=8] {'col'}, use_global_device_ids=true, to_apply=%region_10.11 | all-reduce | flops 1 | bytes 8 | tf_op jit(solution)/shard_map/psum | solution.py:86
  354.1 70.8 %all-reduce.22.cloned.1.call-done = f32[65536]{0:T(1024)} async-done(((f32[65536]{0:T(1024)}), f32[65536]{0:T(1024)}) %all-reduce.22.cloned.1.call-update) | async-done | bytes 262160 | tf_op jit(solution)/shard_map/psum | solution.py:103
  426.9 7.8 %fusion.10 = f32[256,1,128]{2,1,0:T(1,128)S(1)} fusion(bf16[1,1,256,128,128]{4,3,2,1,0:T(8,128)(2,1)} %param.10, bf16[256,128,1]{1,0,2:T(8,128)(2,1)S(1)} %bitcast.68), kind=kOutput, calls=%fused_computation.28 | convolution fusion | flops 8388608 | bytes 8585216 | tf_op jit(solution)/shard_map/kij,kj->ki/dot_general | solution.py:110
  434.7 1.7 scatter_custom_fusion.5
  437.2 24.5 %all-gather.5.cloned.1.call-done = f32[8,1,65536]{2,1,0:T(1,128)} async-done(((f32[1,1,65536]{2,1,0:T(1,128)}), f32[8,1,65536]{2,1,0:T(1,128)}) %all-gather.5.cloned.1.call-update) | async-done | bytes 2097168 | tf_op jit(solution)/shard_map/all_gather | solution.py:114
  461.8 3.1 reduce_sum.38
  465.8 5.6 fusion.8
  471.5 1.7 scatter_custom_fusion.6
  474.0 84.8 %all-reduce.24.cloned.1.call-done = f32[65536]{0:T(1024)} async-done(((f32[65536]{0:T(1024)}), f32[65536]{0:T(1024)}) %all-reduce.24.cloned.1.call-update) | async-done | bytes 262160 | tf_op jit(solution)/shard_map/psum | solution.py:103
  558.8 1.9 fusion.40
  561.5 7.8 %fusion.6 = f32[256,1,128]{2,1,0:T(1,128)S(1)} fusion(bf16[1,1,256,128,128]{4,3,2,1,0:T(8,128)(2,1)} %param.10, bf16[256,128,1]{1,0,2:T(8,128)(2,1)S(1)} %bitcast.66), kind=kOutput, calls=%fused_computation.24 | convolution fusion | flops 8388608 | bytes 8585216 | tf_op jit(solution)/shard_map/kij,kj->ki/dot_general | solution.py:110
  569.3 1.7 scatter_custom_fusion.7
  571.7 24.6 %all-gather.7.cloned.1.call-done = f32[8,1,65536]{2,1,0:T(1,128)} async-done(((f32[1,1,65536]{2,1,0:T(1,128)}), f32[8,1,65536]{2,1,0:T(1,128)}) %all-gather.7.cloned.1.call-update) | async-done | bytes 2097168 | tf_op jit(solution)/shard_map/all_gather | solution.py:114
  596.3 3.1 reduce_sum.39
  (75 shorter events, 26.1 us)
Async XLA Ops:
  7.2 79.6 %all-reduce.16.cloned.1.call-start = ((), (), s32[]{:S(2)}) async-start(), calls=%async_computation.1 | async-start | bytes 524288 | tf_op jit(solution)/shard_map/pmax | solution.py:78
  23.9 226.1 %copy-start.3 = (f32[65536]{0:T(1024)S(1)}, f32[65536]{0:T(1024)}, u32[]{:S(2)}) copy-start(f32[65536]{0:T(1024)} %param.14) | copy-start | bytes 786436
  24.0 150.5 %all-reduce.14.cloned.1.call-start = ((), (), s32[]{:S(2)}) async-start(), calls=%async_computation | async-start | bytes 524288 | tf_op jit(solution)/shard_map/pmax | solution.py:79
  26.4 225.3 %copy-start.4 = (f32[65536]{0:T(1024)S(1)}, f32[65536]{0:T(1024)}, u32[]{:S(2)}) copy-start(f32[65536]{0:T(1024)} %param.19) | copy-start | bytes 786436
  26.4 223.5 %all-reduce.20.cloned.1.call-start = ((), (), s32[]{:S(2)}) async-start(), calls=%async_computation.3 | async-start | bytes 524288 | tf_op jit(solution)/shard_map/pmax | solution.py:78
  86.7 163.3 %copy-start.2 = (f32[65536]{0:T(1024)S(1)}, f32[65536]{0:T(1024)}, u32[]{:S(2)}) copy-start(f32[65536]{0:T(1024)} %all-reduce.16.cloned.1.call-done) | copy-start | bytes 786436
  188.1 149.4 %copy-start.1 = (f32[65536]{0:T(1024)S(1)}, f32[65536]{0:T(1024)}, u32[]{:S(2)}) copy-start(f32[65536]{0:T(1024)} %all-reduce.14.cloned.1.call-done) | copy-start | bytes 786436
  188.2 149.4 %copy-start.5 = (f32[65536]{0:T(1024)S(1)}, f32[65536]{0:T(1024)}, u32[]{:S(2)}) copy-start(f32[65536]{0:T(1024)} %param.13) | copy-start | bytes 786436
  188.2 236.7 %copy-start.6 = (f32[65536]{0:T(1024)S(1)}, f32[65536]{0:T(1024)}, u32[]{:S(2)}) copy-start(f32[65536]{0:T(1024)} %param.18) | copy-start | bytes 786436
  188.2 236.7 %copy-start.7 = (f32[65536]{0:T(1024)S(1)}, f32[65536]{0:T(1024)}, u32[]{:S(2)}) copy-start(f32[65536]{0:T(1024)} %param.15) | copy-start | bytes 786436
  188.2 236.7 %copy-start.8 = (s32[65536]{0:T(1024)S(1)}, s32[65536]{0:T(1024)}, u32[]{:S(2)}) copy-start(s32[65536]{0:T(1024)} %param.17) | copy-start | bytes 786436
  188.2 236.6 %copy-start.9 = (f32[65536]{0:T(1024)S(1)}, f32[65536]{0:T(1024)}, u32[]{:S(2)}) copy-start(f32[65536]{0:T(1024)} %param.16) | copy-start | bytes 786436
  190.6 147.0 %all-reduce.18.cloned.1.call-start = ((), (), s32[]{:S(2)}) async-start(), calls=%async_computation.2 | async-start | bytes 524288 | tf_op jit(solution)/shard_map/pmax | solution.py:79
  193.1 231.7 %all-reduce.22.cloned.1.call-start = ((), (), s32[]{:S(2)}) async-start(), calls=%async_computation.4 | async-start | bytes 524288 | tf_op jit(solution)/shard_map/psum | solution.py:103
  260.7 201.1 %all-gather.5.cloned.1.call-start = ((), (), s32[]{:S(2)}) async-start(), calls=%async_computation.6 | async-start | bytes 2359296 | tf_op jit(solution)/shard_map/all_gather | solution.py:114
  434.7 124.0 %copy-start = (f32[65536]{0:T(1024)S(1)}, f32[65536]{0:T(1024)}, u32[]{:S(2)}) copy-start(f32[65536]{0:T(1024)} %all-reduce.22.cloned.1.call-done) | copy-start | bytes 786436
  437.2 121.6 %all-reduce.24.cloned.1.call-start = ((), (), s32[]{:S(2)}) async-start(), calls=%async_computation.5 | async-start | bytes 524288 | tf_op jit(solution)/shard_map/psum | solution.py:103
  473.9 122.4 %all-gather.7.cloned.1.call-start = ((), (), s32[]{:S(2)}) async-start(), calls=%async_computation.7 | async-start | bytes 2359296 | tf_op jit(solution)/shard_map/all_gather | solution.py:114
Sparse Core Ops, SparseCore 0:
  24.1 62.5 all-reduce.15
  90.8 83.6 all-reduce.13
  190.8 59.1 all-reduce.19
  253.9 83.6 all-reduce.17
  341.2 83.6 all-reduce.21
  437.3 24.4 all-gather.4
  474.0 84.6 all-reduce.23
  571.8 24.4 all-gather.6
